TPU v7x, 32 devices: a whole 2x2x4 slice. The times are simulated.
32 devices in a mesh: dp: 16 (over z, y, core), mp: 2 (over x).
Axes of the slice: x: 2, y: 2, z: 4, core: 2. Of those that a mesh axis runs over, the one named last changes fastest.
Arguments:
- tokens: bfloat16 [16384, 1024], P('dp', 'mp'), may hold values from -6 to 6
- cotangent: bfloat16 [16384, 1024], P('dp', 'mp'), may hold values from -6 to 6
- route: int32 [16384], P('dp'), may hold values from 0 to 16383, as said below
- seq_lengths: int32 [16, 4], P('dp'), may hold values from 1 to 512, 1024 in all within a row
- norm1_gain: float32 [1024], replicated, may hold values from 0.25 to 1.75
- in_weight: bfloat16 [3, 1024, 1024], P(None, None, 'mp'), may hold values from -0.1875 to 0.1875
- conv_weight: float32 [3, 1024], P(None, 'mp'), may hold values from -3 to 3
- out_weight: bfloat16 [1024, 1024], P('mp'), may hold values from -0.1875 to 0.1875
- norm2_gain: float32 [1024], replicated, may hold values from 0.25 to 1.75
- gate_weight: bfloat16 [1024, 4608], P(None, 'mp'), may hold values from -0.1875 to 0.1875
- up_weight: bfloat16 [1024, 4608], P(None, 'mp'), may hold values from -0.1875 to 0.1875
- down_weight: bfloat16 [4608, 1024], P('mp'), may hold values from -0.09375 to 0.09375
Outputs:
- block_out: bfloat16 [16384, 1024], P('dp', 'mp')
- tokens_grad: float32 [16384, 1024], P('dp', 'mp')
- norm1_gain_grad: float32 [1024], replicated
- in_weight_grad: float32 [3, 1024, 1024], P(None, None, 'mp')
- conv_weight_grad: float32 [3, 1024], P(None, 'mp')
- out_weight_grad: float32 [1024, 1024], P('mp')
- norm2_gain_grad: float32 [1024], replicated
- gate_weight_grad: float32 [1024, 4608], P(None, 'mp')
- up_weight_grad: float32 [1024, 4608], P(None, 'mp')
- down_weight_grad: float32 [4608, 1024], P('mp')
Inputs may be any that keep to these rules, and one draw needn't show every extreme that they name: route is a permutation of the packed places; the 1024 arrival rows of one dp shard go 96 to one group, 32 to another and 64 to each other group, which groups drawn from the seed. `seq_lengths`: each row sums to 1024.
All inputs are finite; a program needn't handle non-finite values.
Results may differ from a plain program's by a relative error of at most 0.011.
Values may be sent and summed in bfloat16 or wider, within the bound.
No kernel may reach another device: no remote copies, remote signals or barrier semaphores. Data moves between devices by JAX's collectives and lax.ppermute only.
A program may use at most 192 MiB of HBM per device.

v0:
```python
import jax
import jax.numpy as jnp
from jax import lax
from jax.sharding import PartitionSpec as P

epsilon = 1e-05


def lag_rows(values, shift):
    return jnp.concatenate(
        [jnp.zeros((shift, values.shape[1]), values.dtype), values[:-shift]], axis=0
    )


def lead_rows(values, shift):
    return jnp.concatenate(
        [values[shift:], jnp.zeros((shift, values.shape[1]), values.dtype)], axis=0
    )


def seq_masks(lengths, row_count):
    starts = jnp.cumsum(lengths, dtype=jnp.int32) - lengths
    position = jnp.arange(row_count, dtype=jnp.int32)
    started = position[:, None] >= starts[None, :]
    seq_first = jnp.max(jnp.where(started, starts[None, :], 0), axis=1)
    offset = position - seq_first
    return ((offset >= 1).astype(jnp.float32)[:, None], (offset >= 2).astype(jnp.float32)[:, None])


def padded_piece(piece, start, model_width):
    return lax.dynamic_update_slice_in_dim(jnp.zeros((model_width,), jnp.float32), piece, start, 0)


def on_device(
    tokens,
    cotangent,
    route,
    seq_lengths,
    norm1_gain,
    in_weight,
    conv_weight,
    out_weight,
    norm2_gain,
    gate_weight,
    up_weight,
    down_weight,
):
    dp_size = lax.axis_size("dp")
    mp_index = lax.axis_index("mp")
    row_count = tokens.shape[0]
    narrow = tokens.shape[1]
    model_width = norm1_gain.shape[0]
    pair_share = row_count // dp_size
    slot_count = pair_share + pair_share // 2
    ordering = jnp.argsort(route)
    target = route[ordering] // row_count
    members = jnp.arange(dp_size, dtype=jnp.int32)
    counts = jnp.sum(
        (target[:, None] == members[None, :]).astype(jnp.int32), axis=0, dtype=jnp.int32
    )
    begins = jnp.cumsum(counts, dtype=jnp.int32) - counts
    slot_ids = jnp.arange(slot_count, dtype=jnp.int32)
    filled = slot_ids[None, :] < counts[:, None]
    sources = ordering[jnp.clip(begins[:, None] + slot_ids[None, :], 0, row_count - 1)]
    pulled_rows = tokens[sources]
    pulled_seeds = cotangent[sources]
    send_rows = jnp.where(filled[:, :, None], pulled_rows, jnp.zeros_like(pulled_rows))
    send_seeds = jnp.where(filled[:, :, None], pulled_seeds, jnp.zeros_like(pulled_seeds))
    send_places = jnp.where(filled, route[sources] % row_count, row_count)
    got_rows, got_seeds, got_places = (
        lax.all_to_all(send_rows, "dp", split_axis=0, concat_axis=0, tiled=True),
        lax.all_to_all(send_seeds, "dp", split_axis=0, concat_axis=0, tiled=True),
        lax.all_to_all(send_places, "dp", split_axis=0, concat_axis=0, tiled=True),
    )
    flat_places = got_places.reshape(-1)
    input_piece = (
        jnp.zeros((row_count, narrow), tokens.dtype)
        .at[flat_places]
        .set(got_rows.reshape(-1, narrow), mode="drop")
    )
    seed_piece = (
        jnp.zeros((row_count, narrow), cotangent.dtype)
        .at[flat_places]
        .set(got_seeds.reshape(-1, narrow), mode="drop")
    )
    input_full, seed_full = (
        lax.all_gather(input_piece, "mp", axis=1, tiled=True),
        lax.all_gather(seed_piece, "mp", axis=1, tiled=True),
    )
    first_mask, second_mask = seq_masks(seq_lengths[0], row_count)
    column_start = mp_index * narrow
    gain_one = lax.dynamic_slice_in_dim(norm1_gain, column_start, narrow)
    gain_two = lax.dynamic_slice_in_dim(norm2_gain, column_start, narrow)
    residual = input_full.astype(jnp.float32)
    residual_piece = input_piece.astype(jnp.float32)
    scale_one = lax.rsqrt(jnp.mean(residual * residual, axis=1) + epsilon)
    normed_one = (residual * scale_one[:, None] * norm1_gain).astype(jnp.bfloat16)
    projected = jnp.einsum("rd,kdc->krc", normed_one, in_weight, preferred_element_type=jnp.float32)
    in_gate, out_gate, value_part = (projected[0], projected[1], projected[2])
    mixed = in_gate * value_part
    lag_one = lag_rows(mixed, 1) * first_mask
    lag_two = lag_rows(mixed, 2) * second_mask
    convolved = conv_weight[2] * mixed + conv_weight[1] * lag_one + conv_weight[0] * lag_two
    gated = (out_gate * convolved).astype(jnp.bfloat16)
    mix_terms = jnp.dot(gated, out_weight, preferred_element_type=jnp.float32)
    middle = residual_piece + lax.psum_scatter(mix_terms, "mp", scatter_dimension=1, tiled=True)
    square_sum = lax.psum(jnp.sum(middle * middle, axis=1), "mp")
    scale_two = lax.rsqrt(square_sum / model_width + epsilon)
    normed_piece = (middle * scale_two[:, None] * gain_two).astype(jnp.bfloat16)
    normed_two = lax.all_gather(normed_piece, "mp", axis=1, tiled=True)
    gate_val = jnp.dot(normed_two, gate_weight, preferred_element_type=jnp.float32)
    up_val = jnp.dot(normed_two, up_weight, preferred_element_type=jnp.float32)
    sigmoid_val = jax.nn.sigmoid(gate_val)
    silu_val = gate_val * sigmoid_val
    hidden = (silu_val * up_val).astype(jnp.bfloat16)
    down_terms = jnp.dot(hidden, down_weight, preferred_element_type=jnp.float32)
    block_piece = middle + lax.psum_scatter(down_terms, "mp", scatter_dimension=1, tiled=True)
    seed_local = seed_piece.astype(jnp.float32)
    grad_down = jnp.einsum("rf,rd->fd", hidden, seed_full, preferred_element_type=jnp.float32)
    grad_hidden = jnp.einsum(
        "rd,fd->rf", seed_full, down_weight, preferred_element_type=jnp.float32
    )
    grad_gate_val = (
        grad_hidden * up_val * sigmoid_val * (1.0 + gate_val * (1.0 - sigmoid_val))
    ).astype(jnp.bfloat16)
    grad_up_val = (grad_hidden * silu_val).astype(jnp.bfloat16)
    grad_gate = jnp.einsum(
        "rd,rf->df", normed_two, grad_gate_val, preferred_element_type=jnp.float32
    )
    grad_up = jnp.einsum("rd,rf->df", normed_two, grad_up_val, preferred_element_type=jnp.float32)
    normed_terms = jnp.einsum(
        "rf,df->rd", grad_gate_val, gate_weight, preferred_element_type=jnp.float32
    ) + jnp.einsum("rf,df->rd", grad_up_val, up_weight, preferred_element_type=jnp.float32)
    grad_normed_two = lax.psum_scatter(normed_terms, "mp", scatter_dimension=1, tiled=True)
    gain_two_piece = jnp.sum(grad_normed_two * middle * scale_two[:, None], axis=0)
    dot_two, grad_gain_two = lax.psum(
        (
            jnp.sum(gain_two * grad_normed_two * middle, axis=1),
            padded_piece(gain_two_piece, column_start, model_width),
        ),
        "mp",
    )
    grad_middle = (
        seed_local
        + scale_two[:, None] * gain_two * grad_normed_two
        - middle * (scale_two * scale_two * scale_two * dot_two / model_width)[:, None]
    )
    grad_mix_piece = grad_middle.astype(jnp.bfloat16)
    grad_mix = lax.all_gather(grad_mix_piece, "mp", axis=1, tiled=True)
    grad_out_weight = jnp.einsum("rc,rd->cd", gated, grad_mix, preferred_element_type=jnp.float32)
    grad_gated = jnp.einsum("rd,cd->rc", grad_mix, out_weight, preferred_element_type=jnp.float32)
    grad_conv = grad_gated * out_gate
    grad_conv_weight = jnp.stack(
        [
            jnp.sum(grad_conv * lag_two, axis=0),
            jnp.sum(grad_conv * lag_one, axis=0),
            jnp.sum(grad_conv * mixed, axis=0),
        ],
        axis=0,
    )
    grad_mixed = (
        conv_weight[2] * grad_conv
        + conv_weight[1] * lead_rows(grad_conv * first_mask, 1)
        + conv_weight[0] * lead_rows(grad_conv * second_mask, 2)
    )
    grad_parts = jnp.stack(
        [grad_mixed * value_part, grad_gated * convolved, grad_mixed * in_gate], axis=0
    ).astype(jnp.bfloat16)
    grad_in_weight = jnp.einsum(
        "rd,krc->kdc", normed_one, grad_parts, preferred_element_type=jnp.float32
    )
    first_terms = jnp.einsum(
        "krc,kdc->rd", grad_parts, in_weight, preferred_element_type=jnp.float32
    )
    grad_normed_one = lax.psum_scatter(first_terms, "mp", scatter_dimension=1, tiled=True)
    gain_one_piece = jnp.sum(grad_normed_one * residual_piece * scale_one[:, None], axis=0)
    dot_one, grad_gain_one = lax.psum(
        (
            jnp.sum(gain_one * grad_normed_one * residual_piece, axis=1),
            padded_piece(gain_one_piece, column_start, model_width),
        ),
        "mp",
    )
    input_grad = (
        grad_middle
        + scale_one[:, None] * gain_one * grad_normed_one
        - residual_piece * (scale_one * scale_one * scale_one * dot_one / model_width)[:, None]
    )
    summed = lax.psum(
        (
            grad_gain_one,
            grad_in_weight,
            grad_conv_weight,
            grad_out_weight,
            grad_gain_two,
            grad_gate,
            grad_up,
            grad_down,
        ),
        "dp",
    )
    local_ids = jnp.clip(got_places, 0, row_count - 1)
    back_out, back_grad = (
        lax.all_to_all(block_piece[local_ids], "dp", split_axis=0, concat_axis=0, tiled=True),
        lax.all_to_all(input_grad[local_ids], "dp", split_axis=0, concat_axis=0, tiled=True),
    )
    home = jnp.where(filled, sources, row_count).reshape(-1)
    block_out = (
        jnp.zeros((row_count, narrow), jnp.float32)
        .at[home]
        .set(back_out.reshape(-1, narrow), mode="drop")
        .astype(jnp.bfloat16)
    )
    tokens_grad = (
        jnp.zeros((row_count, narrow), jnp.float32)
        .at[home]
        .set(back_grad.reshape(-1, narrow), mode="drop")
    )
    return (
        block_out,
        tokens_grad,
        summed[0],
        summed[1],
        summed[2],
        summed[3],
        summed[4],
        summed[5],
        summed[6],
        summed[7],
    )


def solution(mesh):
    in_specs = (
        P("dp", "mp"),
        P("dp", "mp"),
        P("dp"),
        P("dp", None),
        P(),
        P(None, None, "mp"),
        P(None, "mp"),
        P("mp", None),
        P(),
        P(None, "mp"),
        P(None, "mp"),
        P("mp", None),
    )
    out_specs = (
        P("dp", "mp"),
        P("dp", "mp"),
        P(),
        P(None, None, "mp"),
        P(None, "mp"),
        P("mp", None),
        P(),
        P(None, "mp"),
        P(None, "mp"),
        P("mp", None),
    )
    return jax.shard_map(
        on_device, mesh=mesh, in_specs=in_specs, out_specs=out_specs, check_vma=False
    )
```

profile of v0, /device:TPU:0, one launch (start us, length us, event | category | flops | bytes accessed | tf_op | source)
XLA Modules:
  0.0 1352.7 jit_solution(5558362743720589754)
XLA Ops:
  30.7 7.4 all-to-all-start
  38.2 6.8 gather_fusion.5
  63.2 30.1 %all-to-all-done.1 = bf16[16,96,512]{2,1,0:T(8,128)(2,1)} async-done(((bf16[16,96,512]{2,1,0:T(8,128)(2,1)}), bf16[16,96,512]{2,1,0:T(8,128)(2,1)}, u32[]{:S(2)}, u32[]{:S(2)}) %all-to-all-start.1) | async-done | bytes 1572896 | tf_op jit(solution)/shard_map/all_to_all | solution.py:71
  93.3 8.7 scatter_custom_fusion
  102.6 37.1 %all-gather.5.cloned.1.call-done = bf16[1024,1024]{1,0:T(8,128)(2,1)} async-done(((bf16[1024,512]{1,0:T(8,128)(2,1)}), bf16[1024,1024]{1,0:T(8,128)(2,1)}) %all-gather.5.cloned.1.call-update) | async-done | bytes 2097168 | tf_op jit(solution)/shard_map/all_gather | solution.py:87
  160.9 48.6 %reduce-scatter.5.cloned.1.call-done = f32[1024,512]{1,0:T(8,128)} async-done(((f32[1024,1024]{1,0:T(8,128)}), f32[1024,512]{1,0:T(8,128)}) %reduce-scatter.5.cloned.1.call-update) | async-done | bytes 2097168 | tf_op jit(solution)/shard_map/reduce_scatter | solution.py:106
  220.8 8.7 scatter_custom_fusion.2
  229.8 24.2 %all-gather.7.cloned.1.call-done = bf16[1024,1024]{1,0:T(8,128)(2,1)} async-done(((bf16[1024,512]{1,0:T(8,128)(2,1)}), bf16[1024,1024]{1,0:T(8,128)(2,1)}) %all-gather.7.cloned.1.call-update) | async-done | bytes 2097168 | tf_op jit(solution)/shard_map/all_gather | solution.py:110
  254.0 10.2 fusion.41
  264.2 9.9 fusion.40
  274.1 14.5 %all-gather.9.cloned.1.call-done = bf16[1024,1024]{1,0:T(8,128)(2,1)} async-done(((bf16[1024,512]{1,0:T(8,128)(2,1)}), bf16[1024,1024]{1,0:T(8,128)(2,1)}) %all-gather.9.cloned.1.call-update) | async-done | bytes 2097168 | tf_op jit(solution)/shard_map/all_gather | solution.py:88
  288.6 17.8 %multiply_convert_fusion = (bf16[1024,2304]{1,0:T(8,128)(2,1)}, bf16[1024,2304]{1,0:T(8,128)(2,1)}, bf16[1024,2304]{1,0:T(8,128)(2,1)}) fusion(f32[1024,2304]{1,0:T(8,128)} %fusion.40, f32[1024,2304]{1,0:T(8,128)} %fusion.41, bf16[1024,1024]{1,0:T(8,128)(2,1)} %all-gather.9.cloned.1.call-done, bf16[2304,1024]{1,0:T(8,128)(2,1)} %param.23), kind=kOutput, calls=%fused_computation.11 | convolution fusion | flops 4867227648 | bytes 39845888 | tf_op jit(solution)/shard_map/rd,fd->rf/dot_general | solution.py:120
  306.4 8.5 fusion.43
  314.9 9.0 convolution_add_fusion
  324.0 54.4 %reduce-scatter.9.cloned.1.call-done = f32[1024,512]{1,0:T(8,128)} async-done(((f32[1024,1024]{1,0:T(8,128)}), f32[1024,512]{1,0:T(8,128)}) %reduce-scatter.9.cloned.1.call-update) | async-done | bytes 2097168 | tf_op jit(solution)/shard_map/reduce_scatter | solution.py:134
  390.8 33.1 %all-gather.11.cloned.1.call-done = bf16[1024,1024]{1,0:T(8,128)(2,1)} async-done(((bf16[1024,512]{1,0:T(8,128)(2,1)}), bf16[1024,1024]{1,0:T(8,128)(2,1)}) %all-gather.11.cloned.1.call-update) | async-done | bytes 2097168 | tf_op jit(solution)/shard_map/all_gather | solution.py:149
  423.9 7.0 multiply_reduce_fusion.3
  442.6 9.7 fusion.42
  452.6 10.3 fusion.47
  462.9 10.2 fusion.46
  473.1 10.3 fusion.45
  499.8 7.1 all-reduce.6
  506.9 46.9 %reduce-scatter.7.cloned.1.call-done = f32[1024,512]{1,0:T(8,128)} async-done(((f32[1024,1024]{1,0:T(8,128)}), f32[1024,512]{1,0:T(8,128)}) %reduce-scatter.7.cloned.1.call-update) | async-done | bytes 2097168 | tf_op jit(solution)/shard_map/reduce_scatter | solution.py:117
  559.1 7.3 gather_fusion.4
  577.0 91.2 %all-to-all-done.2 = f32[16,96,512]{2,1,0:T(8,128)} async-done(((f32[16,96,512]{2,1,0:T(8,128)}), f32[16,96,512]{2,1,0:T(8,128)}, u32[]{:S(2)}, u32[]{:S(2)}) %all-to-all-start.2) | async-done | bytes 3145760 | tf_op jit(solution)/shard_map/all_to_all | solution.py:204
  668.2 12.8 all-to-all-start.4
  681.3 143.8 %all-reduce.4 = (f32[1024]{0:T(1024)}, f32[3,512]{1,0:T(4,128)}, f32[1024]{0:T(1024)}) all-reduce(f32[1024]{0:T(1024)S(1)} %get-tuple-element.68, f32[3,512]{1,0:T(4,128)S(1)} %pad_maximum_fusion.3, f32[1024]{0:T(1024)S(1)} %get-tuple-element.69), channel_id=1, replica_groups=mesh['dp'=16,'mp'=2] {'dp'}, use_global_device_ids=true, to_apply=%region_22.23 | all-reduce | flops 3584 | bytes 28672 | tf_op jit(solution)/shard_map/psum | solution.py:189
  825.1 8.1 scatter_custom_fusion.1
  834.3 9.0 scatter_custom_fusion.3
  843.3 473.7 %all-reduce.9.cloned.1.call-done = (f32[3,1024,512]{1,2,0:T(8,128)}, f32[512,1024]{1,0:T(8,128)}, f32[1024,2304]{1,0:T(8,128)}, f32[1024,2304]{1,0:T(8,128)}, f32[2304,1024]{1,0:T(8,128)}) async-done(((f32[3,1024,512]{1,2,0:T(8,128)}, f32[512,1024]{1,0:T(8,128)}, f32[1024,2304]{1,0:T(8,128)}, f32[1024,2304]{1,0:T(8,128)}, f32[2304,1024]{1,0:T(8,128)}), (f32[3,1024,512]{1,2,0:T(8,128)}, ...) | async-done | bytes 36700176 | tf_op jit(solution)/shard_map/psum | solution.py:189
  1325.1 8.4 copy.45
  1333.5 8.1 copy.46
  (178 shorter events, 145.0 us)
Async XLA Ops:
  7.2 134.9 %copy-start = (bf16[3,1024,512]{2,1,0:T(8,128)(2,1)S(1)}, bf16[3,1024,512]{2,1,0:T(8,128)(2,1)}, u32[]{:S(2)}) copy-start(bf16[3,1024,512]{2,1,0:T(8,128)(2,1)} %param.17) | copy-start | bytes 9437188
  17.1 21.0 %copy-start.24 = (s32[16]{0:T(128)}, s32[16]{0:T(128)S(1)}, u32[]{:S(2)}) copy-start(s32[16]{0:T(128)S(1)} %convert_reduce_fusion) | copy-start | bytes 196
  30.7 24.4 %all-to-all-start = ((s32[16,1,96]{2,1,0:T(1,128)}), s32[16,1,96]{2,1,0:T(1,128)S(1)}, u32[]{:S(2)}, u32[]{:S(2)}) async-start(s32[16,1,96]{2,1,0:T(1,128)} %compare_select_fusion.4), calls=%async_computation | async-start | bytes 16384 | tf_op jit(solution)/shard_map/all_to_all | solution.py:73
  55.1 47.2 %copy-start.32 = (s32[1,4]{1,0:T(1,128)S(1)}, s32[1,4]{1,0:T(1,128)}, u32[]{:S(2)}) copy-start(s32[1,4]{1,0:T(1,128)} %param.15) | copy-start | bytes 52
  55.1 47.5 %copy-start.26 = (f32[3,512]{1,0:T(4,128)S(1)}, f32[3,512]{1,0:T(4,128)}, u32[]{:S(2)}) copy-start(f32[3,512]{1,0:T(4,128)} %param.18) | copy-start | bytes 18436
  55.1 38.2 %all-to-all-start.1 = ((bf16[16,96,512]{2,1,0:T(8,128)(2,1)}), bf16[16,96,512]{2,1,0:T(8,128)(2,1)}, u32[]{:S(2)}, u32[]{:S(2)}) async-start(bf16[16,96,512]{2,1,0:T(8,128)(2,1)} %get-tuple-element.91), calls=%async_computation.1 | async-start | bytes 3145728 | tf_op jit(solution)/shard_map/all_to_all | solution.py:71
  61.3 78.5 %all-gather.5.cloned.1.call-start = ((), (), s32[]{:S(2)}) async-start(), calls=%async_computation.9 | async-start | bytes 3145728 | tf_op jit(solution)/shard_map/all_gather | solution.py:87
  93.3 48.7 %copy-start.28 = (f32[1024]{0:T(1024)S(1)}, f32[1024]{0:T(1024)}, u32[]{:S(2)}) copy-start(f32[1024]{0:T(1024)} %param.16) | copy-start | bytes 12292
  102.1 107.4 %reduce-scatter.5.cloned.1.call-start = ((), (), s32[]{:S(2)}) async-start(), calls=%async_computation.10 | async-start | bytes 6291456 | tf_op jit(solution)/shard_map/reduce_scatter | solution.py:106
  155.0 65.7 %all-to-all-start.3 = ((bf16[16,96,512]{2,1,0:T(8,128)(2,1)}), bf16[16,96,512]{2,1,0:T(8,128)(2,1)}, u32[]{:S(2)}, u32[]{:S(2)}) async-start(bf16[16,96,512]{2,1,0:T(8,128)(2,1)} %get-tuple-element.90), calls=%async_computation.5 | async-start | bytes 3145728 | tf_op jit(solution)/shard_map/all_to_all | solution.py:72
  160.7 93.3 %all-gather.7.cloned.1.call-start = ((), (), s32[]{:S(2)}) async-start(), calls=%async_computation.11 | async-start | bytes 3145728 | tf_op jit(solution)/shard_map/all_gather | solution.py:110
  220.7 67.9 %all-gather.9.cloned.1.call-start = ((), (), s32[]{:S(2)}) async-start(), calls=%async_computation.13 | async-start | bytes 3145728 | tf_op jit(solution)/shard_map/all_gather | solution.py:88
  229.5 148.9 %reduce-scatter.9.cloned.1.call-start = ((), (), s32[]{:S(2)}) async-start(), calls=%async_computation.14 | async-start | bytes 6291456 | tf_op jit(solution)/shard_map/reduce_scatter | solution.py:134
  254.0 10.2 copy-start.29
  306.4 8.5 copy-start.33
  323.9 99.9 %all-gather.11.cloned.1.call-start = ((), (), s32[]{:S(2)}) async-start(), calls=%async_computation.15 | async-start | bytes 3145728 | tf_op jit(solution)/shard_map/all_gather | solution.py:149
  390.6 106.5 %reduce-scatter.11.cloned.1.call-start = ((), (), s32[]{:S(2)}) async-start(), calls=%async_computation.16 | async-start | bytes 6291456 | tf_op jit(solution)/shard_map/reduce_scatter | solution.py:175
  442.6 111.2 %reduce-scatter.7.cloned.1.call-start = ((), (), s32[]{:S(2)}) async-start(), calls=%async_computation.12 | async-start | bytes 6291456 | tf_op jit(solution)/shard_map/reduce_scatter | solution.py:117
  452.3 10.5 copy-start.30
  452.4 864.7 %all-reduce.9.cloned.1.call-start = ((), (), s32[]{:S(2)}) async-start(), calls=%async_computation.17 | async-start | bytes 73400320 | tf_op jit(solution)/shard_map/psum | solution.py:189
  462.9 10.2 copy-start.31
  473.1 10.3 copy-start.6
  473.1 10.3 copy-start.8
  492.2 14.6 %copy-start.22 = (f32[1024]{0:T(1024)S(1)}, f32[1024]{0:T(1024)}, u32[]{:S(2)}) copy-start(f32[1024]{0:T(1024)} %copy-done.21) | copy-start | bytes 12292
  566.4 101.8 %all-to-all-start.2 = ((f32[16,96,512]{2,1,0:T(8,128)}), f32[16,96,512]{2,1,0:T(8,128)}, u32[]{:S(2)}, u32[]{:S(2)}) async-start(f32[16,96,512]{2,1,0:T(8,128)} %bitcast.104), calls=%async_computation.4 | async-start | bytes 6291456 | tf_op jit(solution)/shard_map/all_to_all | solution.py:204
  668.2 12.8 copy-start.20
  668.2 12.9 copy-start.25
  668.2 166.1 %all-to-all-start.4 = ((f32[16,96,512]{2,1,0:T(8,128)}), f32[16,96,512]{2,1,0:T(8,128)}, u32[]{:S(2)}, u32[]{:S(2)}) async-start(f32[16,96,512]{2,1,0:T(8,128)} %bitcast.103), calls=%async_computation.8 | async-start | bytes 6291456 | tf_op jit(solution)/shard_map/all_to_all | solution.py:205
  1317.1 6.7 copy-start.11
  1325.1 16.5 %slice-start = ((s8[9437184]{0:T(1024)(128)(4,1)}), s8[4194304]{0:T(1024)(128)(4,1)S(1)}, s32[]{:S(2)}) async-start(s8[9437184]{0:T(1024)(128)(4,1)} %bitcast.105), calls=%async_computation.18 | async-start | bytes 8388608
  1325.1 16.5 %slice-start.1 = ((s8[9437184]{0:T(1024)(128)(4,1)}), s8[4194304]{0:T(1024)(128)(4,1)S(1)}, s32[]{:S(2)}) async-start(s8[9437184]{0:T(1024)(128)(4,1)} %bitcast.105), calls=%async_computation.19 | async-start | bytes 8388608
  1333.5 8.1 slice-start.2
  (19 other events, 59.1 us)
Sparse Core Ops, SparseCore 0:
  102.2 37.5 all-gather.4
  155.1 54.2 reduce-scatter.4
  220.8 33.1 all-gather.6
  255.5 33.1 all-gather.8
  324.1 54.3 reduce-scatter.8
  390.7 33.1 all-gather.10
  442.7 54.3 reduce-scatter.10
  499.5 54.2 reduce-scatter.6
  560.2 756.7 all-reduce.8
where the time goes:
time: 1360 us; the launch traced here: 1350 us
  waiting for transfers between devices  858 us (63%)
  blocking collectives  161 us (12%)
  matrix products  123 us (9%)
  local copies, waits for them, and re-layouts  113 us (8%)
  other arithmetic  44 us (3%)
  starting transfers between devices  38.6 us (3%)
  between operations  14.6 us (1%)
    psum x1, waiting for transfers between devices, on_device(): lax.psum((grad_gain_one, grad_in_weight, grad_conv_weight, grad_out_weigh...  474 us
    psum x1, blocking collectives, on_device(): lax.psum((grad_gain_one, grad_in_weight, grad_conv_weight, grad_out_weigh...  144 us
    all_to_all x1, waiting for transfers between devices, on_device(): lax.all_to_all(block_piece[local_ids], 'dp', split_axis=0, concat_axis=0,...  91.2 us
    reduce_scatter x1, waiting for transfers between devices, on_device(): lax.psum_scatter(normed_terms, 'mp', scatter_dimension=1, tiled=True)  54.4 us
    reduce_scatter x1, waiting for transfers between devices, on_device(): lax.psum_scatter(mix_terms, 'mp', scatter_dimension=1, tiled=True)  48.6 us
    reduce_scatter x1, waiting for transfers between devices, on_device(): lax.psum_scatter(down_terms, 'mp', scatter_dimension=1, tiled=True)  46.9 us
    all_gather x1, waiting for transfers between devices, on_device(): lax.all_gather(input_piece, 'mp', axis=1, tiled=True)  37.1 us
    unnamed x79, local copies, waits for them, and re-layouts  34.7 us
  transfers between devices with their start and end apart: 14, of which 11 were waited for; matrix products, arithmetic and copies ran while one was open for 11% of the time, Pallas kernels for 0%

commit v1 on v0

--- a/solution.py
+++ b/solution.py
@@ -4,6 +4,22 @@
 from jax.sharding import PartitionSpec as P
 
 epsilon = 1e-05
+
+
+def pairwise_exchange(x, axis, split, join):
+    ways, here = (lax.axis_size(axis), lax.axis_index(axis))
+    width = x.shape[split] // ways
+    shape = list(x.shape)
+    shape[split] = width
+    height = shape[join]
+    shape[join] = height * ways
+    full = jnp.zeros(shape, x.dtype)
+    for mask in range(ways):
+        part = lax.dynamic_slice_in_dim(x, (here ^ mask) * width, width, axis=split)
+        if mask:
+            part = lax.ppermute(part, axis, [(d, d ^ mask) for d in range(ways)])
+        full = lax.dynamic_update_slice_in_dim(full, part, (here ^ mask) * height, axis=join)
+    return full
 
 
 def lag_rows(values, shift):
@@ -201,7 +217,7 @@
     )
     local_ids = jnp.clip(got_places, 0, row_count - 1)
     back_out, back_grad = (
-        lax.all_to_all(block_piece[local_ids], "dp", split_axis=0, concat_axis=0, tiled=True),
+        pairwise_exchange(block_piece[local_ids], "dp", 0, 0),
         lax.all_to_all(input_grad[local_ids], "dp", split_axis=0, concat_axis=0, tiled=True),
     )
     home = jnp.where(filled, sources, row_count).reshape(-1)

time: 1360 us -> 1370 us (level)
  waiting for transfers between devices: 858 us -> 822 us
  blocking collectives: 161 us -> 180 us
  local copies, waits for them, and re-layouts: 113 us -> 129 us
    all_to_all x1 -> x0, waiting for transfers between devices: 91.2 us -> none  [on_device(): lax.all_to_all(block_piece[local_ids], 'dp', split_axis=0, concat_axis=0,...]
    ppermute x0 -> x15, waiting for transfers between devices: none -> 73.2 us  [pairwise_exchange(): part = lax.ppermute(part, axis, [(d, d ^ mask) for d in range(ways)])]
    ppermute x0 -> x15, starting transfers between devices: none -> 19.7 us  [pairwise_exchange(): part = lax.ppermute(part, axis, [(d, d ^ mask) for d in range(ways)])]
    psum x1, blocking collectives: 144 us -> 162 us  [on_device(): lax.psum((grad_gain_one, grad_in_weight, grad_conv_weight, grad_out_weigh...]
    psum x1, waiting for transfers between devices: 474 us -> 457 us  [on_device(): lax.psum((grad_gain_one, grad_in_weight, grad_conv_weight, grad_out_weigh...]
    unnamed x79 -> x93, local copies, waits for them, and re-layouts: 34.7 us -> 37.9 us
  transfers between devices with their start and end apart: 14 -> 28, of which waited for: 11 -> 19; matrix products, arithmetic and copies ran while one was open for 11% -> 11% of each run, Pallas kernels for 0% -> 0%
where the time goes in v1:
time: 1370 us; the launch traced here: 1360 us
  waiting for transfers between devices  822 us (60%)
  blocking collectives  180 us (13%)
  local copies, waits for them, and re-layouts  129 us (9%)
  matrix products  123 us (9%)
  starting transfers between devices  45.7 us (3%)
  other arithmetic  44 us (3%)
  between operations  14.7 us (1%)
    psum x1, waiting for transfers between devices, on_device(): lax.psum((grad_gain_one, grad_in_weight, grad_conv_weight, grad_out_weigh...  457 us
    psum x1, blocking collectives, on_device(): lax.psum((grad_gain_one, grad_in_weight, grad_conv_weight, grad_out_weigh...  162 us
    ppermute x15, waiting for transfers between devices, pairwise_exchange(): part = lax.ppermute(part, axis, [(d, d ^ mask) for d in range(ways)])  73.2 us
    reduce_scatter x1, waiting for transfers between devices, on_device(): lax.psum_scatter(normed_terms, 'mp', scatter_dimension=1, tiled=True)  54.4 us
    reduce_scatter x1, waiting for transfers between devices, on_device(): lax.psum_scatter(mix_terms, 'mp', scatter_dimension=1, tiled=True)  48.6 us
    reduce_scatter x1, waiting for transfers between devices, on_device(): lax.psum_scatter(down_terms, 'mp', scatter_dimension=1, tiled=True)  46.3 us
    unnamed x93, local copies, waits for them, and re-layouts  37.9 us
    all_gather x1, waiting for transfers between devices, on_device(): lax.all_gather(input_piece, 'mp', axis=1, tiled=True)  37.1 us
  transfers between devices with their start and end apart: 28, of which 19 were waited for; matrix products, arithmetic and copies ran while one was open for 11% of the time, Pallas kernels for 0%

profile of v1, /device:TPU:0, one launch (start us, length us, event | category | flops | bytes accessed | tf_op | source)
XLA Modules:
  0.0 1359.0 jit_solution(17710249508894525925)
XLA Ops:
  63.2 30.1 %all-to-all-done.1 = bf16[16,96,512]{2,1,0:T(8,128)(2,1)} async-done(((bf16[16,96,512]{2,1,0:T(8,128)(2,1)}), bf16[16,96,512]{2,1,0:T(8,128)(2,1)}, u32[]{:S(2)}, u32[]{:S(2)}) %all-to-all-start.1) | async-done | bytes 1572896 | tf_op jit(solution)/shard_map/all_to_all | solution.py:87
  93.3 8.7 scatter_custom_fusion
  102.6 37.1 %all-gather.5.cloned.1.call-done = bf16[1024,1024]{1,0:T(8,128)(2,1)} async-done(((bf16[1024,512]{1,0:T(8,128)(2,1)}), bf16[1024,1024]{1,0:T(8,128)(2,1)}) %all-gather.5.cloned.1.call-update) | async-done | bytes 2097168 | tf_op jit(solution)/shard_map/all_gather | solution.py:103
  160.8 48.6 %reduce-scatter.5.cloned.1.call-done = f32[1024,512]{1,0:T(8,128)} async-done(((f32[1024,1024]{1,0:T(8,128)}), f32[1024,512]{1,0:T(8,128)}) %reduce-scatter.5.cloned.1.call-update) | async-done | bytes 2097168 | tf_op jit(solution)/shard_map/reduce_scatter | solution.py:122
  220.7 8.8 scatter_custom_fusion.2
  229.7 24.2 %all-gather.7.cloned.1.call-done = bf16[1024,1024]{1,0:T(8,128)(2,1)} async-done(((bf16[1024,512]{1,0:T(8,128)(2,1)}), bf16[1024,1024]{1,0:T(8,128)(2,1)}) %all-gather.7.cloned.1.call-update) | async-done | bytes 2097168 | tf_op jit(solution)/shard_map/all_gather | solution.py:126
  253.9 10.2 fusion.41
  264.1 9.9 fusion.40
  274.1 14.5 %all-gather.9.cloned.1.call-done = bf16[1024,1024]{1,0:T(8,128)(2,1)} async-done(((bf16[1024,512]{1,0:T(8,128)(2,1)}), bf16[1024,1024]{1,0:T(8,128)(2,1)}) %all-gather.9.cloned.1.call-update) | async-done | bytes 2097168 | tf_op jit(solution)/shard_map/all_gather | solution.py:104
  288.5 17.9 %multiply_convert_fusion = (bf16[1024,2304]{1,0:T(8,128)(2,1)}, bf16[1024,2304]{1,0:T(8,128)(2,1)}, bf16[1024,2304]{1,0:T(8,128)(2,1)}) fusion(f32[1024,2304]{1,0:T(8,128)} %fusion.40, f32[1024,2304]{1,0:T(8,128)} %fusion.41, bf16[1024,1024]{1,0:T(8,128)(2,1)} %all-gather.9.cloned.1.call-done, bf16[2304,1024]{1,0:T(8,128)(2,1)} %param.23), kind=kOutput, calls=%fused_computation.11 | convolution fusion | flops 4867227648 | bytes 39845888 | tf_op jit(solution)/shard_map/rd,fd->rf/dot_general | solution.py:136
  306.4 8.5 fusion.43
  314.9 9.0 convolution_add_fusion
  324.0 54.4 %reduce-scatter.9.cloned.1.call-done = f32[1024,512]{1,0:T(8,128)} async-done(((f32[1024,1024]{1,0:T(8,128)}), f32[1024,512]{1,0:T(8,128)}) %reduce-scatter.9.cloned.1.call-update) | async-done | bytes 2097168 | tf_op jit(solution)/shard_map/reduce_scatter | solution.py:150
  390.8 33.1 %all-gather.11.cloned.1.call-done = bf16[1024,1024]{1,0:T(8,128)(2,1)} async-done(((bf16[1024,512]{1,0:T(8,128)(2,1)}), bf16[1024,1024]{1,0:T(8,128)(2,1)}) %all-gather.11.cloned.1.call-update) | async-done | bytes 2097168 | tf_op jit(solution)/shard_map/all_gather | solution.py:165
  423.8 7.5 multiply_reduce_fusion.3
  443.1 9.6 fusion.42
  453.0 10.3 fusion.47
  463.3 10.2 fusion.46
  473.5 10.3 fusion.45
  500.2 7.7 all-reduce.6
  507.9 46.3 %reduce-scatter.7.cloned.1.call-done = f32[1024,512]{1,0:T(8,128)} async-done(((f32[1024,1024]{1,0:T(8,128)}), f32[1024,512]{1,0:T(8,128)}) %reduce-scatter.7.cloned.1.call-update) | async-done | bytes 2097168 | tf_op jit(solution)/shard_map/reduce_scatter | solution.py:133
  592.7 162.3 %all-reduce.4 = (f32[1024]{0:T(1024)}, f32[3,512]{1,0:T(4,128)}, f32[1024]{0:T(1024)}) all-reduce(f32[1024]{0:T(1024)} %get-tuple-element.68, f32[3,512]{1,0:T(4,128)S(1)} %pad_maximum_fusion.3, f32[1024]{0:T(1024)} %get-tuple-element.69), channel_id=1, replica_groups=mesh['dp'=16,'mp'=2] {'dp'}, use_global_device_ids=true, to_apply=%region_22.23 | all-reduce | flops 3584 | bytes 28672 | tf_op jit(solution)/shard_map/psum | solution.py:205
  778.5 7.7 collective-permute-done.5
  788.4 7.8 collective-permute-done.6
  804.4 14.8 %collective-permute-done.8 = f32[1,96,512]{2,1,0:T(8,128)S(1)} collective-permute-done((f32[1,96,512]{2,1,0:T(8,128)S(1)}, f32[1,96,512]{2,1,0:T(8,128)S(1)}, u32[]{:S(2)}, u32[]{:S(2)}) %collective-permute-start.8) | collective-permute-done | bytes 196640 | tf_op jit(solution)/shard_map/ppermute | solution.py:20
  819.9 14.1 %collective-permute-done.9 = f32[1,96,512]{2,1,0:T(8,128)S(1)} collective-permute-done((f32[1,96,512]{2,1,0:T(8,128)S(1)}, f32[1,96,512]{2,1,0:T(8,128)S(1)}, u32[]{:S(2)}, u32[]{:S(2)}) %collective-permute-start.9) | collective-permute-done | bytes 196640 | tf_op jit(solution)/shard_map/ppermute | solution.py:20
  836.9 8.3 collective-permute-done.10
  848.7 8.1 scatter_custom_fusion.1
  857.8 9.0 scatter_custom_fusion.3
  866.8 456.6 %all-reduce.9.cloned.1.call-done = (f32[3,1024,512]{1,2,0:T(8,128)}, f32[512,1024]{1,0:T(8,128)}, f32[1024,2304]{1,0:T(8,128)}, f32[1024,2304]{1,0:T(8,128)}, f32[2304,1024]{1,0:T(8,128)}) async-done(((f32[3,1024,512]{1,2,0:T(8,128)}, f32[512,1024]{1,0:T(8,128)}, f32[1024,2304]{1,0:T(8,128)}, f32[1024,2304]{1,0:T(8,128)}, f32[2304,1024]{1,0:T(8,128)}), (f32[3,1024,512]{1,2,0:T(8,128)}, ...) | async-done | bytes 36700176 | tf_op jit(solution)/shard_map/psum | solution.py:205
  1331.5 8.4 copy.61
  1339.8 8.1 copy.62
  (237 shorter events, 222.1 us)
Async XLA Ops:
  30.7 24.4 %all-to-all-start = ((s32[16,1,96]{2,1,0:T(1,128)}), s32[16,1,96]{2,1,0:T(1,128)S(1)}, u32[]{:S(2)}, u32[]{:S(2)}) async-start(s32[16,1,96]{2,1,0:T(1,128)} %compare_select_fusion.4), calls=%async_computation | async-start | bytes 16384 | tf_op jit(solution)/shard_map/all_to_all | solution.py:89
  55.1 38.2 %all-to-all-start.1 = ((bf16[16,96,512]{2,1,0:T(8,128)(2,1)}), bf16[16,96,512]{2,1,0:T(8,128)(2,1)}, u32[]{:S(2)}, u32[]{:S(2)}) async-start(bf16[16,96,512]{2,1,0:T(8,128)(2,1)} %get-tuple-element.107), calls=%async_computation.1 | async-start | bytes 3145728 | tf_op jit(solution)/shard_map/all_to_all | solution.py:87
  61.3 78.5 %all-gather.5.cloned.1.call-start = ((), (), s32[]{:S(2)}) async-start(), calls=%async_computation.8 | async-start | bytes 3145728 | tf_op jit(solution)/shard_map/all_gather | solution.py:103
  102.1 107.3 %reduce-scatter.5.cloned.1.call-start = ((), (), s32[]{:S(2)}) async-start(), calls=%async_computation.9 | async-start | bytes 6291456 | tf_op jit(solution)/shard_map/reduce_scatter | solution.py:122
  155.0 65.7 %all-to-all-start.2 = ((bf16[16,96,512]{2,1,0:T(8,128)(2,1)}), bf16[16,96,512]{2,1,0:T(8,128)(2,1)}, u32[]{:S(2)}, u32[]{:S(2)}) async-start(bf16[16,96,512]{2,1,0:T(8,128)(2,1)} %get-tuple-element.106), calls=%async_computation.4 | async-start | bytes 3145728 | tf_op jit(solution)/shard_map/all_to_all | solution.py:88
  160.7 93.2 %all-gather.7.cloned.1.call-start = ((), (), s32[]{:S(2)}) async-start(), calls=%async_computation.10 | async-start | bytes 3145728 | tf_op jit(solution)/shard_map/all_gather | solution.py:126
  220.6 67.9 %all-gather.9.cloned.1.call-start = ((), (), s32[]{:S(2)}) async-start(), calls=%async_computation.12 | async-start | bytes 3145728 | tf_op jit(solution)/shard_map/all_gather | solution.py:104
  229.5 148.9 %reduce-scatter.9.cloned.1.call-start = ((), (), s32[]{:S(2)}) async-start(), calls=%async_computation.13 | async-start | bytes 6291456 | tf_op jit(solution)/shard_map/reduce_scatter | solution.py:150
  323.9 99.9 %all-gather.11.cloned.1.call-start = ((), (), s32[]{:S(2)}) async-start(), calls=%async_computation.14 | async-start | bytes 3145728 | tf_op jit(solution)/shard_map/all_gather | solution.py:165
  390.6 106.9 %reduce-scatter.11.cloned.1.call-start = ((), (), s32[]{:S(2)}) async-start(), calls=%async_computation.15 | async-start | bytes 6291456 | tf_op jit(solution)/shard_map/reduce_scatter | solution.py:191
  443.0 111.2 %reduce-scatter.7.cloned.1.call-start = ((), (), s32[]{:S(2)}) async-start(), calls=%async_computation.11 | async-start | bytes 6291456 | tf_op jit(solution)/shard_map/reduce_scatter | solution.py:133
  452.7 870.7 %all-reduce.9.cloned.1.call-start = ((), (), s32[]{:S(2)}) async-start(), calls=%async_computation.16 | async-start | bytes 73400320 | tf_op jit(solution)/shard_map/psum | solution.py:205
  566.9 291.0 %all-to-all-start.3 = ((f32[16,96,512]{2,1,0:T(8,128)}), f32[16,96,512]{2,1,0:T(8,128)}, u32[]{:S(2)}, u32[]{:S(2)}) async-start(f32[16,96,512]{2,1,0:T(8,128)} %bitcast.103), calls=%async_computation.7 | async-start | bytes 6291456 | tf_op jit(solution)/shard_map/all_to_all | solution.py:221
  583.0 213.2 %copy-start.24 = (f32[1,96,512]{2,1,0:T(8,128)S(1)}, f32[1,96,512]{2,1,0:T(8,128)}, u32[]{:S(2)}) copy-start(f32[1,96,512]{2,1,0:T(8,128)} %get-tuple-element.86) | copy-start | bytes 589828
  583.0 219.3 %copy-start.23 = (f32[1,96,512]{2,1,0:T(8,128)S(1)}, f32[1,96,512]{2,1,0:T(8,128)}, u32[]{:S(2)}) copy-start(f32[1,96,512]{2,1,0:T(8,128)} %get-tuple-element.85) | copy-start | bytes 589828
  583.0 236.2 %copy-start.22 = (f32[1,96,512]{2,1,0:T(8,128)S(1)}, f32[1,96,512]{2,1,0:T(8,128)}, u32[]{:S(2)}) copy-start(f32[1,96,512]{2,1,0:T(8,128)} %get-tuple-element.84) | copy-start | bytes 589828
  583.0 251.0 %copy-start.21 = (f32[1,96,512]{2,1,0:T(8,128)S(1)}, f32[1,96,512]{2,1,0:T(8,128)}, u32[]{:S(2)}) copy-start(f32[1,96,512]{2,1,0:T(8,128)} %get-tuple-element.83) | copy-start | bytes 589828
  583.0 171.9 %collective-permute-start = (f32[1,96,512]{2,1,0:T(8,128)}, f32[1,96,512]{2,1,0:T(8,128)S(1)}, u32[]{:S(2)}, u32[]{:S(2)}) collective-permute-start(f32[1,96,512]{2,1,0:T(8,128)} %get-tuple-element.94), channel_id=1, source_target_pairs={{0,2},{2,0},{4,6},{6,4},{8,10},{10,8},{12,14},{14,12},{16,18},{18,... | collective-permute-start | bytes 589832 | tf_op jit(solution)/shard_map/ppermute | solution.py:20
  583.4 172.3 %collective-permute-start.1 = (f32[1,96,512]{2,1,0:T(8,128)}, f32[1,96,512]{2,1,0:T(8,128)S(1)}, u32[]{:S(2)}, u32[]{:S(2)}) collective-permute-start(f32[1,96,512]{2,1,0:T(8,128)} %get-tuple-element.93), channel_id=1, source_target_pairs={{0,4},{2,6},{4,0},{6,2},{8,12},{10,14},{12,8},{14,10},{16,20},{18,... | collective-permute-start | bytes 589832 | tf_op jit(solution)/shard_map/ppermute | solution.py:20
  585.2 262.8 %collective-permute-start.14 = (f32[1,96,512]{2,1,0:T(8,128)S(1)}, f32[1,96,512]{2,1,0:T(8,128)S(1)}, u32[]{:S(2)}, u32[]{:S(2)}) collective-permute-start(f32[1,96,512]{2,1,0:T(8,128)S(1)} %get-tuple-element.80), channel_id=1, source_target_pairs={{0,30},{2,28},{4,26},{6,24},{8,22},{10,20},{12,18},{14,16},{16,14}... | collective-permute-start | bytes 589832 | tf_op jit(solution)/shard_map/ppermute | solution.py:20
  588.2 259.1 %collective-permute-start.13 = (f32[1,96,512]{2,1,0:T(8,128)S(1)}, f32[1,96,512]{2,1,0:T(8,128)S(1)}, u32[]{:S(2)}, u32[]{:S(2)}) collective-permute-start(f32[1,96,512]{2,1,0:T(8,128)S(1)} %get-tuple-element.81), channel_id=1, source_target_pairs={{0,28},{2,30},{4,24},{6,26},{8,20},{10,22},{12,16},{14,18},{16,12}... | collective-permute-start | bytes 589832 | tf_op jit(solution)/shard_map/ppermute | solution.py:20
  589.6 256.9 %collective-permute-start.12 = (f32[1,96,512]{2,1,0:T(8,128)}, f32[1,96,512]{2,1,0:T(8,128)S(1)}, u32[]{:S(2)}, u32[]{:S(2)}) collective-permute-start(f32[1,96,512]{2,1,0:T(8,128)} %get-tuple-element.82), channel_id=1, source_target_pairs={{0,26},{2,24},{4,30},{6,28},{8,18},{10,16},{12,22},{14,20},{16,10}... | collective-permute-start | bytes 589832 | tf_op jit(solution)/shard_map/ppermute | solution.py:20
  755.0 5.8 collective-permute-start.2
  755.7 14.1 %collective-permute-start.3 = (f32[1,96,512]{2,1,0:T(8,128)}, f32[1,96,512]{2,1,0:T(8,128)S(1)}, u32[]{:S(2)}, u32[]{:S(2)}) collective-permute-start(f32[1,96,512]{2,1,0:T(8,128)} %get-tuple-element.91), channel_id=1, source_target_pairs={{0,8},{2,10},{4,12},{6,14},{8,0},{10,2},{12,4},{14,6},{16,24},{18,... | collective-permute-start | bytes 589832 | tf_op jit(solution)/shard_map/ppermute | solution.py:20
  760.8 17.1 %collective-permute-start.4 = (f32[1,96,512]{2,1,0:T(8,128)}, f32[1,96,512]{2,1,0:T(8,128)S(1)}, u32[]{:S(2)}, u32[]{:S(2)}) collective-permute-start(f32[1,96,512]{2,1,0:T(8,128)} %get-tuple-element.90), channel_id=1, source_target_pairs={{0,10},{2,8},{4,14},{6,12},{8,2},{10,0},{12,6},{14,4},{16,26},{18,... | collective-permute-start | bytes 589832 | tf_op jit(solution)/shard_map/ppermute | solution.py:20
  769.8 16.5 %collective-permute-start.5 = (f32[1,96,512]{2,1,0:T(8,128)}, f32[1,96,512]{2,1,0:T(8,128)S(1)}, u32[]{:S(2)}, u32[]{:S(2)}) collective-permute-start(f32[1,96,512]{2,1,0:T(8,128)} %get-tuple-element.89), channel_id=1, source_target_pairs={{0,12},{2,14},{4,8},{6,10},{8,4},{10,6},{12,0},{14,2},{16,28},{18,... | collective-permute-start | bytes 589832 | tf_op jit(solution)/shard_map/ppermute | solution.py:20
  777.8 18.4 %collective-permute-start.6 = (f32[1,96,512]{2,1,0:T(8,128)}, f32[1,96,512]{2,1,0:T(8,128)S(1)}, u32[]{:S(2)}, u32[]{:S(2)}) collective-permute-start(f32[1,96,512]{2,1,0:T(8,128)} %get-tuple-element.88), channel_id=1, source_target_pairs={{0,14},{2,12},{4,10},{6,8},{8,6},{10,4},{12,2},{14,0},{16,30},{18,... | collective-permute-start | bytes 589832 | tf_op jit(solution)/shard_map/ppermute | solution.py:20
  786.3 16.0 %collective-permute-start.7 = (f32[1,96,512]{2,1,0:T(8,128)}, f32[1,96,512]{2,1,0:T(8,128)S(1)}, u32[]{:S(2)}, u32[]{:S(2)}) collective-permute-start(f32[1,96,512]{2,1,0:T(8,128)} %get-tuple-element.87), channel_id=1, source_target_pairs={{0,16},{2,18},{4,20},{6,22},{8,24},{10,26},{12,28},{14,30},{16,0},... | collective-permute-start | bytes 589832 | tf_op jit(solution)/shard_map/ppermute | solution.py:20
  796.3 23.0 %collective-permute-start.8 = (f32[1,96,512]{2,1,0:T(8,128)S(1)}, f32[1,96,512]{2,1,0:T(8,128)S(1)}, u32[]{:S(2)}, u32[]{:S(2)}) collective-permute-start(f32[1,96,512]{2,1,0:T(8,128)S(1)} %copy-done.24), channel_id=1, source_target_pairs={{0,18},{2,16},{4,22},{6,20},{8,26},{10,24},{12,30},{14,28},{16,2},... | collective-permute-start | bytes 589832 | tf_op jit(solution)/shard_map/ppermute | solution.py:20
  802.3 31.7 %collective-permute-start.9 = (f32[1,96,512]{2,1,0:T(8,128)S(1)}, f32[1,96,512]{2,1,0:T(8,128)S(1)}, u32[]{:S(2)}, u32[]{:S(2)}) collective-permute-start(f32[1,96,512]{2,1,0:T(8,128)S(1)} %copy-done.23), channel_id=1, source_target_pairs={{0,20},{2,22},{4,16},{6,18},{8,28},{10,30},{12,24},{14,26},{16,4},... | collective-permute-start | bytes 589832 | tf_op jit(solution)/shard_map/ppermute | solution.py:20
  819.2 25.9 %collective-permute-start.10 = (f32[1,96,512]{2,1,0:T(8,128)S(1)}, f32[1,96,512]{2,1,0:T(8,128)S(1)}, u32[]{:S(2)}, u32[]{:S(2)}) collective-permute-start(f32[1,96,512]{2,1,0:T(8,128)S(1)} %copy-done.22), channel_id=1, source_target_pairs={{0,22},{2,20},{4,18},{6,16},{8,30},{10,28},{12,26},{14,24},{16,6},... | collective-permute-start | bytes 589832 | tf_op jit(solution)/shard_map/ppermute | solution.py:20
  834.0 11.8 collective-permute-start.11
  (40 other events, 502.2 us)
Sparse Core Ops, SparseCore 0:
  102.2 37.5 all-gather.4
  155.1 54.2 reduce-scatter.4
  220.8 33.1 all-gather.6
  255.4 33.1 all-gather.8
  324.0 54.3 reduce-scatter.8
  390.7 33.1 all-gather.10
  443.2 54.2 reduce-scatter.10
  499.9 54.3 reduce-scatter.6
  560.7 762.6 all-reduce.8
